TPU v7x, 32 devices: a whole 2x2x4 slice. The times are simulated.
32 devices in a mesh: shard: 2 (over x), ctx: 4 (over y, core), tp: 4 (over z).
Axes of the slice: x: 2, y: 2, z: 4, core: 2. Of those that a mesh axis runs over, the one named last changes fastest.
Arguments:
- inputs: bfloat16 [2, 2, 4096, 768], P('shard', None, 'ctx'), may hold values from -6 to 6
- lengths: int32 [2, 2], P('shard'), may hold values from 2048 to 4096, as said below
- attn_gain: bfloat16 [768], P('shard'), may hold values from 0.099609375 to 1.8984375
- mlp_gain: bfloat16 [768], P('shard'), may hold values from 0.099609375 to 1.8984375
- qkv_weight: bfloat16 [768, 3, 768], P('shard', None, 'tp'), may hold values from -0.21875 to 0.21875
- attn_weight: bfloat16 [768, 768], P('tp', 'shard'), may hold values from -0.875 to 0.875
- mlp_in_weight: bfloat16 [768, 2, 1152], P('shard', None, 'tp'), may hold values from -0.21875 to 0.21875
- mlp_out_weight: bfloat16 [1152, 768], P('tp', 'shard'), may hold values from -0.1875 to 0.1875
- cotangent: bfloat16 [2, 2, 4096, 768], P('shard', None, 'ctx'), may hold values from -6 to 6
Outputs:
- layer_out: bfloat16 [2, 2, 4096, 768], P('shard', None, 'ctx')
- input_grad: bfloat16 [2, 2, 4096, 768], P('shard', None, 'ctx')
- qkv_grad: float32 [768, 3, 768], P('shard', None, 'tp')
- attn_grad: float32 [768, 768], P('tp', 'shard')
- mlp_in_grad: float32 [768, 2, 1152], P('shard', None, 'tp')
- mlp_out_grad: float32 [1152, 768], P('tp', 'shard')
- attn_gain_grad: float32 [768], P(('shard', 'tp'))
- mlp_gain_grad: float32 [768], P(('shard', 'tp'))
Inputs may be any that keep to these rules, and one draw needn't show every extreme that they name: `lengths`: among the 2 sequences of each index of shard one has length 4096; some sequence has length 2048.
All inputs are finite; a program needn't handle non-finite values.
Results may differ from a plain program's by a relative error of at most 0.017.
Values may be sent and summed in bfloat16 or wider, within the bound.
A program may use at most 192 MiB of HBM per device.

v0:
```python
import math
import jax
import jax.numpy as jnp
from jax import lax
from jax.sharding import PartitionSpec as P

HD = 64
HALF = 64
norm_eps = 1e-05
rope_base = 10000.0
masked_score = -1e30


def padded(cells, sides, width):
    for axis, dim in sides:
        count = lax.axis_size(axis)
        ends = count - 1
        head = lax.slice_in_dim(cells, 0, width, axis=dim)
        tail = lax.slice_in_dim(cells, cells.shape[dim] - width, cells.shape[dim], axis=dim)
        cells = jnp.concatenate(
            [
                lax.ppermute(tail, axis, [(i, (i + 1) % count) for i in range(ends)]),
                cells,
                lax.ppermute(head, axis, [((i + 1) % count, i) for i in range(ends)]),
            ],
            axis=dim,
        )
    return cells


def layer_norm(values, gain_row):
    center = values - jnp.mean(values, axis=-1, keepdims=True)
    variance = jnp.mean(center * center, axis=-1, keepdims=True)
    return center * lax.rsqrt(variance + norm_eps) * gain_row


def rope_tables(positions):
    exponents = jnp.arange(0, HD, 2).astype(jnp.float32) / HD
    inverse = jnp.power(rope_base, -exponents)
    angles = positions[:, None] * inverse[None, :]
    angles = jnp.concatenate([angles, angles], axis=-1)[:, None, :]
    return (jnp.cos(angles), jnp.sin(angles))


def rotate(vector, cosine, sine_table):
    half_size = vector.shape[-1] // 2
    turned = jnp.concatenate([-vector[..., half_size:], vector[..., :half_size]], axis=-1)
    return vector * cosine + turned * sine_table


def geglu(gate_up):
    return jax.nn.gelu(gate_up[..., 0, :], approximate=False) * gate_up[..., 1, :]


def on_device(
    inputs,
    lengths,
    attn_gain,
    mlp_gain,
    qkv_weight,
    attn_weight,
    mlp_in_weight,
    mlp_out_weight,
    cotangent,
):
    gathered = (
        lax.all_gather(qkv_weight, "shard", axis=0, tiled=True),
        lax.all_gather(attn_weight, "shard", axis=1, tiled=True),
        lax.all_gather(mlp_in_weight, "shard", axis=0, tiled=True),
        lax.all_gather(mlp_out_weight, "shard", axis=1, tiled=True),
        lax.all_gather(attn_gain, "shard", axis=0, tiled=True),
        lax.all_gather(mlp_gain, "shard", axis=0, tiled=True),
    )
    qkv_full, attn_full, mlp_in_full, mlp_out_full, attn_gain_low, mlp_gain_low = gathered
    gain_attn = attn_gain_low.astype(jnp.float32)
    gain_mlp = mlp_gain_low.astype(jnp.float32)
    seq_in = inputs[0].astype(jnp.float32)
    batch_count = seq_in.shape[0]
    local_len = seq_in.shape[1]
    tp_width = qkv_full.shape[2]
    local_heads = tp_width // HD
    ext_len = local_len + 2 * HALF
    scaling = 1.0 / math.sqrt(HD)
    query_tile = min(512, local_len)
    tile_count = local_len // query_tile
    key_span = query_tile + 2 * HALF
    ctx_index = lax.axis_index("ctx")
    positions = ctx_index * local_len + jnp.arange(local_len, dtype=jnp.int32)
    seq_lengths = lengths[0]
    valid_rows = (positions[None, :] < seq_lengths[:, None]).astype(jnp.float32)[:, :, None]
    tile_starts = jnp.arange(tile_count, dtype=jnp.int32) * query_tile
    query_pos = (
        ctx_index * local_len
        + tile_starts[:, None]
        + jnp.arange(query_tile, dtype=jnp.int32)[None, :]
    )
    key_pos = (
        ctx_index * local_len
        - HALF
        + tile_starts[:, None]
        + jnp.arange(key_span, dtype=jnp.int32)[None, :]
    )
    distance = query_pos[:, :, None] - key_pos[:, None, :]
    near_keys = (jnp.abs(distance) <= HALF) & (key_pos[:, None, :] >= 0)
    live_keys = (key_pos[None, :, None, :] < seq_lengths[:, None, None, None]) | (distance == 0)[
        None
    ]
    allowed = (near_keys[None] & live_keys)[:, :, None]
    cosine, sine_table = rope_tables(positions.astype(jnp.float32))

    def key_tiles(extended):
        return jnp.stack(
            [
                extended[:, index * query_tile : index * query_tile + key_span]
                for index in range(tile_count)
            ],
            axis=1,
        )

    def untile(tiles):
        total = jnp.zeros((batch_count, ext_len, local_heads, HD), jnp.float32)
        for index in range(tile_count):
            after = ext_len - index * query_tile - key_span
            total = total + jnp.pad(
                tiles[:, index], ((0, 0), (index * query_tile, after), (0, 0), (0, 0))
            )
        return total

    normed_attn, back_norm_attn = jax.vjp(layer_norm, seq_in, gain_attn)
    normed_low = normed_attn.astype(jnp.bfloat16)
    qkv_raw = jnp.einsum("mtd,dcf->mtcf", normed_low, qkv_full, preferred_element_type=jnp.float32)
    heads_raw = qkv_raw.reshape(batch_count, local_len, 3, local_heads, HD)

    def rope_pair(query_raw, key_raw):
        return (rotate(query_raw, cosine, sine_table), rotate(key_raw, cosine, sine_table))

    (query_rot, key_rot), back_rope = jax.vjp(rope_pair, heads_raw[:, :, 0], heads_raw[:, :, 1])
    queries = query_rot.astype(jnp.bfloat16)
    key_value = jnp.stack([key_rot.astype(jnp.bfloat16), heads_raw[:, :, 2].astype(jnp.bfloat16)])
    key_value = key_value.reshape(2, batch_count, local_len, tp_width)
    key_value_ext = padded(key_value, (("ctx", 2),), HALF)
    key_value_ext = key_value_ext.reshape(2, batch_count, ext_len, local_heads, HD)
    keys_tiled = key_tiles(key_value_ext[0])
    values_tiled = key_tiles(key_value_ext[1])
    queries_tiled = queries.reshape(batch_count, tile_count, query_tile, local_heads, HD)

    def masked_scores():
        raw_scores = (
            jnp.einsum(
                "mnqhd,mnkhd->mnhqk", queries_tiled, keys_tiled, preferred_element_type=jnp.float32
            )
            * scaling
        )
        return jnp.where(allowed, raw_scores, masked_score)

    scores = masked_scores()
    top_score = jnp.max(scores, axis=-1, keepdims=True)
    exponent_terms = jnp.exp(scores - top_score)
    denominator = jnp.sum(exponent_terms, axis=-1, keepdims=True)
    soft_low = (exponent_terms / denominator).astype(jnp.bfloat16)
    log_total = top_score + jnp.log(denominator)
    context = jnp.einsum(
        "mnhqk,mnkhd->mnqhd", soft_low, values_tiled, preferred_element_type=jnp.float32
    )
    context_low = context.astype(jnp.bfloat16).reshape(batch_count, local_len, tp_width)
    attn_part = jnp.einsum(
        "mtf,fd->mtd", context_low, attn_full, preferred_element_type=jnp.float32
    )
    attn_out = lax.psum(attn_part, "tp")
    middle = seq_in + attn_out
    normed_mlp, back_norm_mlp = jax.vjp(layer_norm, middle, gain_mlp)
    normed_mlp_low = normed_mlp.astype(jnp.bfloat16)
    gate_up = jnp.einsum(
        "mtd,dcf->mtcf", normed_mlp_low, mlp_in_full, preferred_element_type=jnp.float32
    )
    hidden, back_glu = jax.vjp(geglu, gate_up)
    hidden_low = hidden.astype(jnp.bfloat16)
    mlp_part = jnp.einsum(
        "mtf,fd->mtd", hidden_low, mlp_out_full, preferred_element_type=jnp.float32
    )
    mlp_out = lax.psum(mlp_part.astype(jnp.bfloat16), "tp").astype(jnp.float32)
    layer_out = ((middle + mlp_out) * valid_rows).astype(jnp.bfloat16)[None]
    grad_out = cotangent[0].astype(jnp.float32) * valid_rows
    grad_out_low = grad_out.astype(jnp.bfloat16)
    mlp_out_grad = jnp.einsum(
        "mtf,mtd->fd", hidden_low, grad_out_low, preferred_element_type=jnp.float32
    )
    grad_hidden = jnp.einsum(
        "mtd,fd->mtf", grad_out_low, mlp_out_full, preferred_element_type=jnp.float32
    )
    (grad_gate_up,) = back_glu(grad_hidden)
    grad_gate_low = grad_gate_up.astype(jnp.bfloat16)
    mlp_in_grad = jnp.einsum(
        "mtd,mtcf->dcf", normed_mlp_low, grad_gate_low, preferred_element_type=jnp.float32
    )
    grad_mlp_part = jnp.einsum(
        "mtcf,dcf->mtd", grad_gate_low, mlp_in_full, preferred_element_type=jnp.float32
    )
    grad_normed_mlp = lax.psum(grad_mlp_part, "tp")
    grad_mid_norm, mlp_gain_grad = back_norm_mlp(grad_normed_mlp)
    grad_middle = grad_out + grad_mid_norm
    grad_middle_low = grad_middle.astype(jnp.bfloat16)
    attn_grad = jnp.einsum(
        "mtf,mtd->fd", context_low, grad_middle_low, preferred_element_type=jnp.float32
    )
    grad_context = jnp.einsum(
        "mtd,fd->mtf", grad_middle_low, attn_full, preferred_element_type=jnp.float32
    )
    grad_context = grad_context.astype(jnp.bfloat16).reshape(
        batch_count, tile_count, query_tile, local_heads, HD
    )
    soft_again = jnp.exp(masked_scores() - log_total)
    soft_again_low = soft_again.astype(jnp.bfloat16)
    grad_values = jnp.einsum(
        "mnhqk,mnqhd->mnkhd", soft_again_low, grad_context, preferred_element_type=jnp.float32
    )
    grad_soft = jnp.einsum(
        "mnqhd,mnkhd->mnhqk", grad_context, values_tiled, preferred_element_type=jnp.float32
    )
    row_terms = jnp.sum(soft_again * grad_soft, axis=-1, keepdims=True)
    grad_scores = (soft_again * (grad_soft - row_terms)).astype(jnp.bfloat16)
    grad_queries = (
        jnp.einsum(
            "mnhqk,mnkhd->mnqhd", grad_scores, keys_tiled, preferred_element_type=jnp.float32
        )
        * scaling
    )
    grad_queries = grad_queries.reshape(batch_count, local_len, local_heads, HD)
    grad_keys = (
        jnp.einsum(
            "mnhqk,mnqhd->mnkhd", grad_scores, queries_tiled, preferred_element_type=jnp.float32
        )
        * scaling
    )
    grad_ext = jnp.stack([untile(grad_keys), untile(grad_values)]).reshape(
        2, batch_count, ext_len, tp_width
    )
    rim_pairs = jnp.concatenate([grad_ext[:, :, :HALF], grad_ext[:, :, ext_len - HALF :]], axis=2)
    arrived = padded(rim_pairs, (("ctx", 2),), HALF)
    from_lower = arrived[:, :, :HALF]
    from_upper = arrived[:, :, arrived.shape[2] - HALF :]
    grad_own = grad_ext[:, :, HALF : HALF + local_len]
    grad_own = grad_own + jnp.pad(from_lower, ((0, 0), (0, 0), (0, local_len - HALF), (0, 0)))
    grad_own = grad_own + jnp.pad(from_upper, ((0, 0), (0, 0), (local_len - HALF, 0), (0, 0)))
    grad_key_rot = grad_own[0].reshape(batch_count, local_len, local_heads, HD)
    grad_value_own = grad_own[1].reshape(batch_count, local_len, local_heads, HD)
    grad_query_raw, grad_key_raw = back_rope((grad_queries, grad_key_rot))
    grad_qkv = jnp.stack([grad_query_raw, grad_key_raw, grad_value_own], axis=2)
    grad_qkv_low = grad_qkv.reshape(batch_count, local_len, 3, tp_width).astype(jnp.bfloat16)
    qkv_grad = jnp.einsum(
        "mtd,mtcf->dcf", normed_low, grad_qkv_low, preferred_element_type=jnp.float32
    )
    grad_attn_part = jnp.einsum(
        "mtcf,dcf->mtd", grad_qkv_low, qkv_full, preferred_element_type=jnp.float32
    )
    grad_normed = lax.psum(grad_attn_part, "tp")
    grad_in_norm, attn_gain_grad = back_norm_attn(grad_normed)
    input_grad = (grad_middle + grad_in_norm).astype(jnp.bfloat16)[None]
    partials = (qkv_grad, attn_grad, mlp_in_grad, mlp_out_grad, attn_gain_grad, mlp_gain_grad)
    summed = lax.psum(
        (partials[0], partials[1], partials[2], partials[3], partials[4], partials[5]), "ctx"
    )
    reduced = (
        lax.psum_scatter(summed[0], "shard", scatter_dimension=0, tiled=True),
        lax.psum_scatter(summed[1], "shard", scatter_dimension=1, tiled=True),
        lax.psum_scatter(summed[2], "shard", scatter_dimension=0, tiled=True),
        lax.psum_scatter(summed[3], "shard", scatter_dimension=1, tiled=True),
        lax.psum_scatter(summed[4], "shard", scatter_dimension=0, tiled=True),
        lax.psum_scatter(summed[5], "shard", scatter_dimension=0, tiled=True),
    )
    gain_share = reduced[4].shape[0] // lax.axis_size("tp")
    gain_start = lax.axis_index("tp") * gain_share
    attn_gain_out = lax.dynamic_slice_in_dim(reduced[4], gain_start, gain_share)
    mlp_gain_out = lax.dynamic_slice_in_dim(reduced[5], gain_start, gain_share)
    return (
        layer_out,
        input_grad,
        reduced[0],
        reduced[1],
        reduced[2],
        reduced[3],
        attn_gain_out,
        mlp_gain_out,
    )


def solution(mesh):
    in_specs = (
        P("shard", None, "ctx", None),
        P("shard", None),
        P("shard"),
        P("shard"),
        P("shard", None, "tp"),
        P("tp", "shard"),
        P("shard", None, "tp"),
        P("tp", "shard"),
        P("shard", None, "ctx", None),
    )
    out_specs = (
        P("shard", None, "ctx", None),
        P("shard", None, "ctx", None),
        P("shard", None, "tp"),
        P("tp", "shard"),
        P("shard", None, "tp"),
        P("tp", "shard"),
        P(("shard", "tp")),
        P(("shard", "tp")),
    )
    return jax.shard_map(
        on_device, mesh=mesh, in_specs=in_specs, out_specs=out_specs, check_vma=False
    )
```

profile of v0, /device:TPU:0, one launch (start us, length us, event | category | flops | bytes accessed | tf_op | source)
XLA Modules:
  0.0 1094.5 jit_solution(6729855262283549967)
XLA Ops:
  8.1 5.3 all-gather
  13.5 2.4 convert_reduce_fusion
  17.6 11.8 %all_gather.19 = bf16[768,3,192]{0,2,1:T(8,128)(2,1)S(1)} all-gather(bf16[384,3,192]{0,2,1:T(8,128)(2,1)S(1)} %copy-done.45), channel_id=1, replica_groups=mesh['shard'=2,'ctx'=4,'tp'=4] {'shard'}, dimensions={0}, use_global_device_ids=true | all-gather | bytes 1327104 | tf_op jit(solution)/shard_map/all_gather | solution.py:67
  29.4 2.6 fusion.32
  33.0 3.1 fusion.178
  43.7 3.7 collective-permute-start
  49.4 3.4 squeeze.38
  60.4 7.3 all_gather.20
  67.7 4.4 concatenate.47
  75.9 3.7 fusion.182
  79.7 3.1 fusion
  82.9 2.2 copy-done
  85.1 5.0 fusion.106
  91.9 3.2 reshape.403
  95.1 4.8 fusion.122
  100.6 4.3 all-gather.1
  104.9 6.9 all_gather.23
  111.8 12.6 %all_gather.22 = bf16[768,2,288]{0,2,1:T(8,128)(2,1)} all-gather(bf16[384,2,288]{0,2,1:T(8,128)(2,1)} %param.15), channel_id=1, replica_groups=mesh['shard'=2,'ctx'=4,'tp'=4] {'shard'}, dimensions={0}, use_global_device_ids=true | all-gather | bytes 1327104 | tf_op jit(solution)/shard_map/all_gather | solution.py:69
  124.5 4.5 fusion.37
  129.1 194.1 %all-reduce.23.cloned.1.call-done = f32[2,1024,768]{2,1,0:T(8,128)} async-done(((f32[2,1024,768]{2,1,0:T(8,128)}), f32[2,1024,768]{2,1,0:T(8,128)}) %all-reduce.23.cloned.1.call-update) | async-done | bytes 6291472 | tf_op jit(solution)/shard_map/psum | solution.py:169
  323.2 3.5 fusion.176
  329.3 2.7 fusion.42
  332.0 5.1 multiply_bitcast_fusion
  339.8 4.6 convolution_bitcast_fusion.1
  345.3 6.4 convolution_convert_fusion
  353.6 9.3 fusion.103
  363.9 7.7 fusion.96
  371.7 194.6 %all-reduce.27.cloned.1.call-done = f32[2,1024,768]{2,1,0:T(8,128)} async-done(((f32[2,1024,768]{2,1,0:T(8,128)}), f32[2,1024,768]{2,1,0:T(8,128)}) %all-reduce.27.cloned.1.call-update) | async-done | bytes 6291472 | tf_op jit(solution)/shard_map/psum | solution.py:199
  566.3 6.2 multiply_reduce_fusion.1
  572.5 116.8 %all-reduce.25.cloned.1.call-done = bf16[2,1024,768]{2,1,0:T(8,128)(2,1)} async-done(((bf16[2,1024,768]{2,1,0:T(8,128)(2,1)}), bf16[2,1024,768]{2,1,0:T(8,128)(2,1)}) %all-reduce.25.cloned.1.call-update) | async-done | bytes 3145744 | tf_op jit(solution)/shard_map/psum | solution.py:181
  689.3 8.3 fusion.174
  704.1 3.4 reshape.404
  707.5 14.0 %multiply_reduce_fusion = (f32[2,2,3,512]{3,2,1,0:T(4,128)S(1)}, f32[2,2,3,512,640]{4,3,2,1,0:T(8,128)}) fusion(f32[2,2,3,512,640]{4,3,2,1,0:T(8,128)} %copy-done, f32[2,2,3,512]{3,2,1,0:T(4,128)S(1)} %log_add_fusion, bf16[2,1,640,3,64]{2,4,3,1,0:T(8,128)(2,1)} %copy-done.33, bf16[2,1,640,3,64]{2,4,3,1,0:T(8,128)(2,1)} %copy-done.32, ...), kind=kOutput, calls=%fused_computation.1 | convolution fusion | flops 515598336 | bytes 33275904 | tf_op jit(solution)/shard_map/mnqhd,mnkhd->mnhqk/dot_general | solution.py:217
  722.7 7.4 multiply_convert_fusion
  730.2 2.5 multiply_bitcast_fusion.2
  734.0 4.3 fusion.89
  743.0 2.6 collective-permute-start.2
  757.4 3.5 fusion.99
  761.0 7.3 convolution_bitcast_fusion
  770.3 25.6 %reduce-scatter.5.cloned.1.call-done = f32[384,3,192]{0,2,1:T(8,128)} async-done(((f32[768,3,192]{0,2,1:T(8,128)}), f32[384,3,192]{0,2,1:T(8,128)}) %reduce-scatter.5.cloned.1.call-update) | async-done | bytes 884752 | tf_op jit(solution)/shard_map/reduce_scatter | solution.py:264
  795.9 225.4 %all-reduce.29.cloned.1.call-done = f32[2,1024,768]{2,1,0:T(8,128)} async-done(((f32[2,1024,768]{2,1,0:T(8,128)}), f32[2,1024,768]{2,1,0:T(8,128)}) %all-reduce.29.cloned.1.call-update) | async-done | bytes 6291472 | tf_op jit(solution)/shard_map/psum | solution.py:256
  1021.2 4.0 fusion.21
  1025.9 3.2 fusion.15
  1029.1 5.0 all-reduce.16
  1034.2 6.7 all-reduce.14
  1042.1 9.2 fusion.30
  1051.3 30.6 %all-reduce.31.cloned.1.call-done = (f32[384,3,192]{0,2,1:T(8,128)}, f32[192,384]{1,0:T(8,128)}, f32[384,2,288]{0,2,1:T(8,128)}, f32[288,384]{1,0:T(8,128)}) async-done(((f32[384,3,192]{0,2,1:T(8,128)}, f32[192,384]{1,0:T(8,128)}, f32[384,2,288]{0,2,1:T(8,128)}, f32[288,384]{1,0:T(8,128)}), (f32[384,3,192]{0,2,1:T(8,128)}, f32[192,384]{1,0:T(8,128)}, f32[384,2,288]{0,2,1:T(8,128)}, ...) | async-done | bytes 2506768 | tf_op jit(solution)/shard_map/psum | solution.py:260
  1081.9 2.2 copy.93
  (230 shorter events, 67.9 us)
Async XLA Ops:
  7.2 8.7 copy-start.1
  7.2 316.0 %all-reduce.23.cloned.1.call-start = ((), (), s32[]{:S(2)}) async-start(), calls=%async_computation.4 | async-start | bytes 12582912 | tf_op jit(solution)/shard_map/psum | solution.py:169
  13.4 15.9 %copy-start.54 = (f32[768]{0:T(1024)}, f32[768]{0:T(1024)S(1)}, u32[]{:S(2)}) copy-start(f32[768]{0:T(1024)S(1)} %reshape.411) | copy-start | bytes 9220
  15.9 16.1 %copy-start.46 = (f32[2,1024]{1,0:T(2,128)}, f32[2,1024]{1,0:T(2,128)S(1)}, u32[]{:S(2)}) copy-start(f32[2,1024]{1,0:T(2,128)S(1)} %broadcast_multiply_fusion.5) | copy-start | bytes 24580
  17.6 14.4 %copy-start.52 = (f32[2,1024]{1,0:T(2,128)}, f32[2,1024]{1,0:T(2,128)S(1)}, u32[]{:S(2)}) copy-start(f32[2,1024]{1,0:T(2,128)S(1)} %fusion.130) | copy-start | bytes 24580
  29.4 2.7 copy-start.39
  42.4 25.3 %collective-permute-start.1 = (bf16[2,2,64,192]{2,3,1,0:T(8,128)(2,1)}, bf16[2,2,64,192]{2,3,1,0:T(8,128)(2,1)}, u32[]{:S(2)}, u32[]{:S(2)}) collective-permute-start(bf16[2,2,64,192]{2,3,1,0:T(8,128)(2,1)} %get-tuple-element.43), channel_id=1, source_target_pairs={{4,0},{8,4},{12,8},{5,1},{9,5},{13,9},{6,2},{10,6},{14,10},{7,3},{... | collective-permute-start | bytes 294920 | tf_op jit(solution)/shard_map/ppermute | solution.py:24
  43.7 24.0 %collective-permute-start = (bf16[2,2,64,192]{2,3,1,0:T(8,128)(2,1)}, bf16[2,2,64,192]{2,3,1,0:T(8,128)(2,1)}, u32[]{:S(2)}, u32[]{:S(2)}) collective-permute-start(bf16[2,2,64,192]{2,3,1,0:T(8,128)(2,1)} %get-tuple-element.44), channel_id=1, source_target_pairs={{0,4},{4,8},{8,12},{1,5},{5,9},{9,13},{2,6},{6,10},{10,14},{3,7},{... | collective-permute-start | bytes 294920 | tf_op jit(solution)/shard_map/ppermute | solution.py:22
  55.5 2.1 copy-start.19
  55.5 2.1 copy-start.37
  73.7 2.3 copy-start.36
  73.8 5.9 copy-start.28
  73.8 5.9 copy-start.30
  73.9 8.9 copy-start.32
  74.0 8.9 copy-start.33
  79.7 5.4 copy-start
  82.8 7.3 copy-start.49
  99.9 466.4 %all-reduce.27.cloned.1.call-start = ((), (), s32[]{:S(2)}) async-start(), calls=%async_computation.6 | async-start | bytes 12582912 | tf_op jit(solution)/shard_map/psum | solution.py:199
  111.8 12.7 %copy-start.34 = (bf16[288,768]{1,0:T(8,128)(2,1)}, bf16[288,768]{1,0:T(8,128)(2,1)S(1)}, u32[]{:S(2)}) copy-start(bf16[288,768]{1,0:T(8,128)(2,1)S(1)} %all_gather.23) | copy-start | bytes 1327108
  326.7 2.6 copy-start.3
  326.7 2.6 copy-start.40
  329.3 2.7 copy-start.11
  332.0 5.2 copy-start.6
  344.4 345.0 %all-reduce.25.cloned.1.call-start = ((), (), s32[]{:S(2)}) async-start(), calls=%async_computation.5 | async-start | bytes 6291456 | tf_op jit(solution)/shard_map/psum | solution.py:181
  351.7 418.5 %reduce-scatter.11.cloned.1.call-start = ((), (), s32[]{:S(2)}) async-start(), calls=%async_computation.11 | async-start | bytes 1327104 | tf_op jit(solution)/shard_map/reduce_scatter | solution.py:267
  362.9 407.3 %reduce-scatter.9.cloned.1.call-start = ((), (), s32[]{:S(2)}) async-start(), calls=%async_computation.10 | async-start | bytes 2654208 | tf_op jit(solution)/shard_map/reduce_scatter | solution.py:266
  371.7 398.6 %reduce-scatter.7.cloned.1.call-start = ((), (), s32[]{:S(2)}) async-start(), calls=%async_computation.9 | async-start | bytes 884736 | tf_op jit(solution)/shard_map/reduce_scatter | solution.py:265
  697.6 2.7 copy-start.4
  704.1 17.4 %slice-start = ((s8[15728640]{0:T(1024)(128)(4,1)}), s8[3145728]{0:T(1024)(128)(4,1)S(1)}, s32[]{:S(2)}) async-start(s8[15728640]{0:T(1024)(128)(4,1)} %bitcast.348), calls=%async_computation.13 | async-start | bytes 6291456
  707.5 14.0 %slice-start.1 = ((s8[15728640]{0:T(1024)(128)(4,1)}), s8[4194304]{0:T(1024)(128)(4,1)S(1)}, s32[]{:S(2)}) async-start(s8[15728640]{0:T(1024)(128)(4,1)} %bitcast.348), calls=%async_computation.14 | async-start | bytes 8388608
  707.5 14.0 %slice-start.2 = ((s8[15728640]{0:T(1024)(128)(4,1)}), s8[4194304]{0:T(1024)(128)(4,1)S(1)}, s32[]{:S(2)}) async-start(s8[15728640]{0:T(1024)(128)(4,1)} %bitcast.348), calls=%async_computation.15 | async-start | bytes 8388608
  707.5 15.2 %slice-start.3 = ((s8[15728640]{0:T(1024)(128)(4,1)}), s8[4194304]{0:T(1024)(128)(4,1)S(1)}, s32[]{:S(2)}) async-start(s8[15728640]{0:T(1024)(128)(4,1)} %bitcast.348), calls=%async_computation.16 | async-start | bytes 8388608
  722.7 7.4 copy-start.29
  722.7 7.4 copy-start.31
  742.0 4.9 copy-start.9
  742.0 4.9 copy-start.13
  743.0 5.6 collective-permute-start.2
  745.6 4.5 collective-permute-start.3
  748.5 47.3 %reduce-scatter.5.cloned.1.call-start = ((), (), s32[]{:S(2)}) async-start(), calls=%async_computation.8 | async-start | bytes 2654208 | tf_op jit(solution)/shard_map/reduce_scatter | solution.py:264
  752.3 3.9 copy-start.41
  755.3 2.1 copy-start.55
  760.9 260.3 %all-reduce.29.cloned.1.call-start = ((), (), s32[]{:S(2)}) async-start(), calls=%async_computation.7 | async-start | bytes 12582912 | tf_op jit(solution)/shard_map/psum | solution.py:256
  768.3 313.6 %all-reduce.31.cloned.1.call-start = ((), (), s32[]{:S(2)}) async-start(), calls=%async_computation.12 | async-start | bytes 5013504 | tf_op jit(solution)/shard_map/psum | solution.py:260
  795.9 229.3 %copy-start.51 = (f32[2,1024]{1,0:T(2,128)S(1)}, f32[2,1024]{1,0:T(2,128)}, u32[]{:S(2)}) copy-start(f32[2,1024]{1,0:T(2,128)} %copy-done.50) | copy-start | bytes 24580
  1021.2 4.6 copy-start.5
  1025.9 3.2 copy-start.56
  1081.9 3.9 copy-start.38
  1081.9 4.9 copy-start.44
  (29 other events, 42.0 us)
Sparse Core Ops, SparseCore 0:
  100.0 223.1 all-reduce.22
  344.5 221.7 all-reduce.26
  569.3 120.0 all-reduce.24
  692.0 17.5 reduce-scatter.10
  711.7 28.2 reduce-scatter.8
  748.6 16.0 reduce-scatter.6
  767.6 28.2 reduce-scatter.4
  798.3 222.8 all-reduce.28
  1024.0 57.8 all-reduce.30
where the time goes:
time: 1100 us; the launch traced here: 1090 us
  waiting for transfers between devices  789 us (72%)
  matrix products  88.2 us (8%)
  other arithmetic  76 us (7%)
  blocking collectives  60 us (5%)
  local copies, waits for them, and re-layouts  56.3 us (5%)
  between operations  15.9 us (1%)
    psum x1, waiting for transfers between devices, on_device(): grad_normed = lax.psum(grad_attn_part, 'tp')  225 us
    psum x1, waiting for transfers between devices, on_device(): grad_normed_mlp = lax.psum(grad_mlp_part, 'tp')  195 us
    psum x1, waiting for transfers between devices, on_device(): attn_out = lax.psum(attn_part, 'tp')  194 us
    psum x1, waiting for transfers between devices, on_device(): mlp_out = lax.psum(mlp_part.astype(jnp.bfloat16), 'tp').astype(jnp.float32)  117 us
    psum x1, waiting for transfers between devices, on_device(): lax.psum((partials[0], partials[1], partials[2], partials[3], partials[4]...  30.6 us
    unnamed x137, local copies, waits for them, and re-layouts  29.4 us
    reduce_scatter x1, waiting for transfers between devices, on_device(): lax.psum_scatter(summed[0], 'shard', scatter_dimension=0, tiled=True)  25.6 us
  transfers between devices with their start and end apart: 13, of which 7 were waited for; matrix products, arithmetic and copies ran while one was open for 12% of the time, Pallas kernels for 0%

commit v1 on v0

--- a/solution.py
+++ b/solution.py
@@ -196,7 +196,8 @@
     grad_mlp_part = jnp.einsum(
         "mtcf,dcf->mtd", grad_gate_low, mlp_in_full, preferred_element_type=jnp.float32
     )
-    grad_normed_mlp = lax.psum(grad_mlp_part, "tp")
+    blocks = lax.all_gather(grad_mlp_part, "tp", axis=0, tiled=False)
+    grad_normed_mlp = blocks.sum(axis=0)
     grad_mid_norm, mlp_gain_grad = back_norm_mlp(grad_normed_mlp)
     grad_middle = grad_out + grad_mid_norm
     grad_middle_low = grad_middle.astype(jnp.bfloat16)

time: 1100 us -> 1310 us (1.19)
  waiting for transfers between devices: 789 us -> 975 us
    all_gather x0 -> x1, waiting for transfers between devices: none -> 395 us  [on_device(): blocks = lax.all_gather(grad_mlp_part, 'tp', axis=0, tiled=False)]
    psum x1 -> x0, waiting for transfers between devices: 195 us -> none  [on_device(): grad_normed_mlp = lax.psum(grad_mlp_part, 'tp')]
    psum x1, waiting for transfers between devices: 117 us -> 103 us  [on_device(): mlp_out = lax.psum(mlp_part.astype(jnp.bfloat16), 'tp').astype(jnp.float32)]
  transfers between devices with their start and end apart: 13 -> 13, of which waited for: 7 -> 7; matrix products, arithmetic and copies ran while one was open for 12% -> 11% of each run, Pallas kernels for 0% -> 0%
where the time goes in v1:
time: 1310 us; the launch traced here: 1300 us
  waiting for transfers between devices  975 us (74%)
  matrix products  89.4 us (7%)
  other arithmetic  88.9 us (7%)
  blocking collectives  60 us (5%)
  local copies, waits for them, and re-layouts  57.1 us (4%)
  between operations  15.9 us (1%)
    all_gather x1, waiting for transfers between devices, on_device(): blocks = lax.all_gather(grad_mlp_part, 'tp', axis=0, tiled=False)  395 us
    psum x1, waiting for transfers between devices, on_device(): grad_normed = lax.psum(grad_attn_part, 'tp')  225 us
    psum x1, waiting for transfers between devices, on_device(): attn_out = lax.psum(attn_part, 'tp')  194 us
    psum x1, waiting for transfers between devices, on_device(): mlp_out = lax.psum(mlp_part.astype(jnp.bfloat16), 'tp').astype(jnp.float32)  103 us
    psum x1, waiting for transfers between devices, on_device(): lax.psum((partials[0], partials[1], partials[2], partials[3], partials[4]...  30.6 us
    unnamed x137, local copies, waits for them, and re-layouts  30.2 us
  transfers between devices with their start and end apart: 13, of which 7 were waited for; matrix products, arithmetic and copies ran while one was open for 11% of the time, Pallas kernels for 0%

profile of v1, /device:TPU:0, one launch (start us, length us, event | category | flops | bytes accessed | tf_op | source)
XLA Modules:
  0.0 1296.2 jit_solution(11746763267222441335)
XLA Ops:
  8.1 5.3 all-gather.1
  13.5 2.4 convert_reduce_fusion
  17.6 11.8 all_gather.25
  29.3 2.6 fusion.32
  33.0 3.1 fusion.178
  43.7 3.7 collective-permute-start
  49.4 3.4 squeeze.38
  60.4 7.3 all_gather.26
  67.7 4.4 concatenate.47
  75.9 3.7 fusion.182
  79.7 3.1 fusion
  85.0 5.0 fusion.106
  91.8 3.3 reshape.403
  95.0 4.9 fusion.122
  100.6 4.3 all-gather.2
  104.9 6.9 all_gather.29
  111.8 12.7 all_gather.28
  124.6 4.5 fusion.37
  129.1 194.1 %all-reduce.22.cloned.1.call-done = f32[2,1024,768]{2,1,0:T(8,128)} async-done(((f32[2,1024,768]{2,1,0:T(8,128)}), f32[2,1024,768]{2,1,0:T(8,128)}) %all-reduce.22.cloned.1.call-update) | async-done | bytes 6291472 | tf_op jit(solution)/shard_map/psum | solution.py:169
  323.2 3.5 fusion.176
  329.4 2.7 fusion.42
  332.1 5.1 multiply_bitcast_fusion
  339.9 4.7 convolution_bitcast_fusion.1
  345.6 6.5 convolution_convert_fusion
  352.1 2.7 copy-done.10
  354.8 9.5 fusion.103
  365.4 8.4 fusion.96
  373.8 395.0 %all-gather.5.cloned.1.call-done = f32[8,1024,768]{2,1,0:T(8,128)} async-done(((f32[2,1024,768]{2,1,0:T(8,128)}), f32[8,1024,768]{2,1,0:T(8,128)}) %all-gather.5.cloned.1.call-update) | async-done | bytes 25165840 | tf_op jit(solution)/shard_map/all_gather | solution.py:199
  768.8 12.9 reduce_sum.121
  781.7 6.3 multiply_reduce_fusion.1
  788.0 103.1 %all-reduce.24.cloned.1.call-done = bf16[2,1024,768]{2,1,0:T(8,128)(2,1)} async-done(((bf16[2,1024,768]{2,1,0:T(8,128)(2,1)}), bf16[2,1024,768]{2,1,0:T(8,128)(2,1)}) %all-reduce.24.cloned.1.call-update) | async-done | bytes 3145744 | tf_op jit(solution)/shard_map/psum | solution.py:181
  891.1 8.3 fusion.174
  905.8 3.4 reshape.404
  909.2 14.0 %multiply_reduce_fusion = (f32[2,2,3,512]{3,2,1,0:T(4,128)S(1)}, f32[2,2,3,512,640]{4,3,2,1,0:T(8,128)}) fusion(f32[2,2,3,512,640]{4,3,2,1,0:T(8,128)} %copy-done, f32[2,2,3,512]{3,2,1,0:T(4,128)S(1)} %log_add_fusion, bf16[2,1,640,3,64]{2,4,3,1,0:T(8,128)(2,1)} %copy-done.33, bf16[2,1,640,3,64]{2,4,3,1,0:T(8,128)(2,1)} %copy-done.32, ...), kind=kOutput, calls=%fused_computation.1 | convolution fusion | flops 515598336 | bytes 33275904 | tf_op jit(solution)/shard_map/mnqhd,mnkhd->mnhqk/dot_general | solution.py:218
  924.4 7.4 multiply_convert_fusion
  931.8 2.5 multiply_bitcast_fusion.2
  935.7 4.3 fusion.89
  944.6 2.6 collective-permute-start.2
  959.0 3.5 fusion.99
  962.6 7.3 convolution_bitcast_fusion
  971.9 25.7 %reduce-scatter.5.cloned.1.call-done = f32[384,3,192]{0,2,1:T(8,128)} async-done(((f32[768,3,192]{0,2,1:T(8,128)}), f32[384,3,192]{0,2,1:T(8,128)}) %reduce-scatter.5.cloned.1.call-update) | async-done | bytes 884752 | tf_op jit(solution)/shard_map/reduce_scatter | solution.py:265
  997.6 225.3 %all-reduce.26.cloned.1.call-done = f32[2,1024,768]{2,1,0:T(8,128)} async-done(((f32[2,1024,768]{2,1,0:T(8,128)}), f32[2,1024,768]{2,1,0:T(8,128)}) %all-reduce.26.cloned.1.call-update) | async-done | bytes 6291472 | tf_op jit(solution)/shard_map/psum | solution.py:257
  1222.9 4.0 fusion.21
  1227.6 3.2 fusion.15
  1230.8 5.0 all-reduce.16
  1235.9 6.7 all-reduce.14
  1243.8 9.2 fusion.30
  1253.0 30.6 %all-reduce.28.cloned.1.call-done = (f32[384,3,192]{0,2,1:T(8,128)}, f32[192,384]{1,0:T(8,128)}, f32[384,2,288]{0,2,1:T(8,128)}, f32[288,384]{1,0:T(8,128)}) async-done(((f32[384,3,192]{0,2,1:T(8,128)}, f32[192,384]{1,0:T(8,128)}, f32[384,2,288]{0,2,1:T(8,128)}, f32[288,384]{1,0:T(8,128)}), (f32[384,3,192]{0,2,1:T(8,128)}, f32[192,384]{1,0:T(8,128)}, f32[384,2,288]{0,2,1:T(8,128)}, ...) | async-done | bytes 2506768 | tf_op jit(solution)/shard_map/psum | solution.py:261
  (231 shorter events, 70.4 us)
Async XLA Ops:
  7.2 8.7 copy-start.1
  7.2 316.1 %all-reduce.22.cloned.1.call-start = ((), (), s32[]{:S(2)}) async-start(), calls=%async_computation.4 | async-start | bytes 12582912 | tf_op jit(solution)/shard_map/psum | solution.py:169
  13.4 15.9 %copy-start.54 = (f32[768]{0:T(1024)}, f32[768]{0:T(1024)S(1)}, u32[]{:S(2)}) copy-start(f32[768]{0:T(1024)S(1)} %reshape.412) | copy-start | bytes 9220
  15.9 16.1 %copy-start.46 = (f32[2,1024]{1,0:T(2,128)}, f32[2,1024]{1,0:T(2,128)S(1)}, u32[]{:S(2)}) copy-start(f32[2,1024]{1,0:T(2,128)S(1)} %broadcast_multiply_fusion.5) | copy-start | bytes 24580
  17.6 14.4 %copy-start.52 = (f32[2,1024]{1,0:T(2,128)}, f32[2,1024]{1,0:T(2,128)S(1)}, u32[]{:S(2)}) copy-start(f32[2,1024]{1,0:T(2,128)S(1)} %fusion.130) | copy-start | bytes 24580
  29.3 2.7 copy-start.39
  42.4 25.3 %collective-permute-start.1 = (bf16[2,2,64,192]{2,3,1,0:T(8,128)(2,1)}, bf16[2,2,64,192]{2,3,1,0:T(8,128)(2,1)}, u32[]{:S(2)}, u32[]{:S(2)}) collective-permute-start(bf16[2,2,64,192]{2,3,1,0:T(8,128)(2,1)} %get-tuple-element.43), channel_id=1, source_target_pairs={{4,0},{8,4},{12,8},{5,1},{9,5},{13,9},{6,2},{10,6},{14,10},{7,3},{... | collective-permute-start | bytes 294920 | tf_op jit(solution)/shard_map/ppermute | solution.py:24
  43.7 24.0 %collective-permute-start = (bf16[2,2,64,192]{2,3,1,0:T(8,128)(2,1)}, bf16[2,2,64,192]{2,3,1,0:T(8,128)(2,1)}, u32[]{:S(2)}, u32[]{:S(2)}) collective-permute-start(bf16[2,2,64,192]{2,3,1,0:T(8,128)(2,1)} %get-tuple-element.44), channel_id=1, source_target_pairs={{0,4},{4,8},{8,12},{1,5},{5,9},{9,13},{2,6},{6,10},{10,14},{3,7},{... | collective-permute-start | bytes 294920 | tf_op jit(solution)/shard_map/ppermute | solution.py:22
  55.5 2.1 copy-start.19
  55.6 2.1 copy-start.37
  73.7 2.3 copy-start.36
  73.8 5.9 copy-start.28
  73.8 5.9 copy-start.30
  73.9 8.9 copy-start.32
  73.9 8.9 copy-start.33
  79.7 5.4 copy-start
  82.8 7.3 copy-start.49
  99.9 668.9 %all-gather.5.cloned.1.call-start = ((), (), s32[]{:S(2)}) async-start(), calls=%async_computation.7 | async-start | bytes 31457280 | tf_op jit(solution)/shard_map/all_gather | solution.py:199
  111.8 12.7 copy-start.34
  326.7 2.7 copy-start.3
  326.7 2.7 copy-start.40
  329.4 2.7 copy-start.11
  332.1 5.2 copy-start.6
  344.6 546.5 %all-reduce.24.cloned.1.call-start = ((), (), s32[]{:S(2)}) async-start(), calls=%async_computation.5 | async-start | bytes 6291456 | tf_op jit(solution)/shard_map/psum | solution.py:181
  352.0 2.8 copy-start.10
  352.1 619.8 %reduce-scatter.11.cloned.1.call-start = ((), (), s32[]{:S(2)}) async-start(), calls=%async_computation.11 | async-start | bytes 1327104 | tf_op jit(solution)/shard_map/reduce_scatter | solution.py:268
  364.4 607.5 %reduce-scatter.9.cloned.1.call-start = ((), (), s32[]{:S(2)}) async-start(), calls=%async_computation.10 | async-start | bytes 2654208 | tf_op jit(solution)/shard_map/reduce_scatter | solution.py:267
  373.8 598.1 %reduce-scatter.7.cloned.1.call-start = ((), (), s32[]{:S(2)}) async-start(), calls=%async_computation.9 | async-start | bytes 884736 | tf_op jit(solution)/shard_map/reduce_scatter | solution.py:266
  899.4 2.6 copy-start.4
  905.8 17.4 %slice-start = ((s8[15728640]{0:T(1024)(128)(4,1)}), s8[3145728]{0:T(1024)(128)(4,1)S(1)}, s32[]{:S(2)}) async-start(s8[15728640]{0:T(1024)(128)(4,1)} %bitcast.349), calls=%async_computation.13 | async-start | bytes 6291456
  909.2 14.0 %slice-start.1 = ((s8[15728640]{0:T(1024)(128)(4,1)}), s8[4194304]{0:T(1024)(128)(4,1)S(1)}, s32[]{:S(2)}) async-start(s8[15728640]{0:T(1024)(128)(4,1)} %bitcast.349), calls=%async_computation.14 | async-start | bytes 8388608
  909.2 14.0 %slice-start.2 = ((s8[15728640]{0:T(1024)(128)(4,1)}), s8[4194304]{0:T(1024)(128)(4,1)S(1)}, s32[]{:S(2)}) async-start(s8[15728640]{0:T(1024)(128)(4,1)} %bitcast.349), calls=%async_computation.15 | async-start | bytes 8388608
  909.2 15.2 %slice-start.3 = ((s8[15728640]{0:T(1024)(128)(4,1)}), s8[4194304]{0:T(1024)(128)(4,1)S(1)}, s32[]{:S(2)}) async-start(s8[15728640]{0:T(1024)(128)(4,1)} %bitcast.349), calls=%async_computation.16 | async-start | bytes 8388608
  924.4 7.4 copy-start.29
  924.4 7.4 copy-start.31
  943.6 4.9 copy-start.9
  943.6 4.9 copy-start.13
  944.6 5.6 collective-permute-start.2
  947.2 4.5 collective-permute-start.3
  950.2 47.3 %reduce-scatter.5.cloned.1.call-start = ((), (), s32[]{:S(2)}) async-start(), calls=%async_computation.8 | async-start | bytes 2654208 | tf_op jit(solution)/shard_map/reduce_scatter | solution.py:265
  954.0 3.9 copy-start.41
  962.5 260.4 %all-reduce.26.cloned.1.call-start = ((), (), s32[]{:S(2)}) async-start(), calls=%async_computation.6 | async-start | bytes 12582912 | tf_op jit(solution)/shard_map/psum | solution.py:257
  969.9 313.7 %all-reduce.28.cloned.1.call-start = ((), (), s32[]{:S(2)}) async-start(), calls=%async_computation.12 | async-start | bytes 5013504 | tf_op jit(solution)/shard_map/psum | solution.py:261
  997.6 229.3 %copy-start.51 = (f32[2,1024]{1,0:T(2,128)S(1)}, f32[2,1024]{1,0:T(2,128)}, u32[]{:S(2)}) copy-start(f32[2,1024]{1,0:T(2,128)} %copy-done.50) | copy-start | bytes 24580
  1222.9 4.6 copy-start.5
  1227.6 3.2 copy-start.56
  1283.6 3.9 copy-start.38
  1283.6 4.9 copy-start.44
  (29 other events, 41.9 us)
Sparse Core Ops, SparseCore 0:
  100.0 223.1 all-reduce.21
  344.7 424.0 all-gather.4
  771.8 119.2 all-reduce.23
  893.8 17.5 reduce-scatter.10
  913.5 28.2 reduce-scatter.8
  950.3 16.0 reduce-scatter.6
  969.3 28.2 reduce-scatter.4
  1000.0 222.8 all-reduce.25
  1225.7 57.8 all-reduce.27
